TPU v7x, 512 devices: a whole 4x8x8 slice. The times are simulated.
512 devices in a mesh: section: 16 (over y, core), expert: 32 (over x, z).
Axes of the slice: x: 4, y: 8, z: 8, core: 2. Of those that a mesh axis runs over, the one named last changes fastest.
Arguments:
- saved_inputs: bfloat16 [16, 2, 256, 2048], P('section', None, 'expert'), may hold values from -6 to 6
- top_grad: bfloat16 [2, 256, 2048], P(None, 'expert'), may hold values from -6 to 6
- expert_ids: int32 [16, 2, 256, 2], P('section', None, 'expert'), may hold values from 0 to 7, all different within a row; in each aligned block of 8 rows (0 to 7, 8 to 15, ..., all dimensions but the last counted through in order) at most 3 rows name the same one
- route_weights: bfloat16 [16, 2, 256, 2], P('section', None, 'expert'), may hold values from 0.099609375 to 0.59765625
- example_ids: int32 [2, 256], P(None, 'expert'), may hold values from 0 to 3, never falling along the last dimension, each value on 1 to 128 neighbouring positions
- gate_weight: bfloat16 [16, 12288, 2048], P('section', 'expert'), may hold values from -0.125 to 0.125
- up_weight: bfloat16 [16, 12288, 2048], P('section', 'expert'), may hold values from -0.125 to 0.125
- down_weight: bfloat16 [16, 12288, 2048], P('section', 'expert'), may hold values from -0.15625 to 0.15625
- left_proj: bfloat16 [16, 12288, 64], P('section', 'expert'), may hold values from -0.15625 to 0.15625
- right_proj: bfloat16 [16, 2048, 64], P('section'), may hold values from -0.125 to 0.125
Outputs:
- input_grads: bfloat16 [16, 2, 256, 2048], P('section', None, 'expert')
- sketches: float32 [16, 64, 4096], P('section', 'expert')
Inputs may be any that keep to these rules, and one draw needn't show every extreme that they name: `expert_ids`: each row names 2 different experts; in each aligned block of 8 rows (one device's tokens of one layer and micro-batch) no expert is named by more than 3 rows, and some block reaches 3. `example_ids`: along each micro-batch the example number never falls and every example has a token.
All inputs are finite; a program needn't handle non-finite values.
Results may differ from a plain program's by a relative error of at most 0.028.
Values may be sent and summed in bfloat16 or wider, within the bound.
A program may use at most 64 MiB of HBM per device.

v0:
```python
import jax
import jax.numpy as jnp
from jax import lax
from jax.sharding import PartitionSpec as P

EXPERTS = 8
EXM = 4
CAP = 3


def in_one_piece(arrays, axis, split_dim, concat_dim, along):
    columns = [a.reshape(*a.shape[:along], -1) for a in arrays]
    both = jnp.concatenate(columns, axis=along)
    filled, at, gathered = (
        lax.all_to_all(both, axis, split_axis=split_dim, concat_axis=concat_dim, tiled=True),
        0,
        [],
    )
    for a, column in zip(arrays, columns):
        slab = filled[..., at : at + column.shape[along]]
        gathered.append(slab.reshape(*slab.shape[:along], *a.shape[along:]))
        at += column.shape[along]
    return tuple(gathered)


def from_behind(block, axis, distance):
    devices = range(lax.axis_size(axis))
    route = [(i - distance, i) for i in devices if i - distance in devices]
    return lax.ppermute(block, axis, route)


def sent_together(arrays, axis, split_dim, concat_dim, along):
    ends, at = ([], 0)
    for a in arrays[:-1]:
        at += a.shape[along]
        ends.append(at)
    both = jnp.concatenate(arrays, axis=along)
    return tuple(
        jnp.split(
            lax.all_to_all(both, axis, split_axis=split_dim, concat_axis=concat_dim, tiled=True),
            ends,
            axis=along,
        )
    )


def in_blocks(x, dim, size):
    before, after = (x.shape[:dim], x.shape[dim + 1 :])
    return jnp.moveaxis(x.reshape(*before, size, -1, *after), dim, 0)


def sent_and_summed(x, axis, dim):
    blocks = in_blocks(x, dim, lax.axis_size(axis))
    arrived = lax.all_to_all(blocks, axis, split_axis=0, concat_axis=0, tiled=True)
    return arrived.sum(axis=0)


def on_device(
    saved_inputs,
    top_grad,
    expert_ids,
    route_weights,
    example_ids,
    gate_weight,
    up_weight,
    down_weight,
    left_proj,
    right_proj,
):
    n_section = lax.axis_size("section")
    n_expert = lax.axis_size("expert")
    section_id = lax.axis_index("section")
    groups = EXPERTS
    hsplit = n_expert // groups
    n_micro = saved_inputs.shape[1]
    tok_dev = saved_inputs.shape[2]
    feat_dim = saved_inputs.shape[3]
    top_k = expert_ids.shape[3]
    n_pairs = tok_dev * top_k
    n_slots = groups * CAP
    n_rows = n_expert * CAP
    sketch_dim = left_proj.shape[2]
    q_total = n_micro * EXM * groups
    inputs = saved_inputs[0]
    ids_flat = expert_ids[0].reshape(n_micro, n_pairs)
    weights_flat = route_weights[0].reshape(n_micro, n_pairs).astype(jnp.float32)
    onehot = (ids_flat[:, :, None] == jnp.arange(groups, dtype=jnp.int32)[None, None, :]).astype(
        jnp.int32
    )
    before = jnp.cumsum(onehot, axis=1) - onehot
    position = jnp.sum(before * onehot, axis=2)
    slot_of = ids_flat * CAP + position
    select = (slot_of[:, None, :] == jnp.arange(n_slots, dtype=jnp.int32)[None, :, None]).astype(
        jnp.float32
    )
    token_select = select.reshape(n_micro, n_slots, tok_dev, top_k).sum(axis=3)
    token_select_b = token_select.astype(jnp.bfloat16)
    slot_weight = jnp.einsum("msp,mp->ms", select, weights_flat, precision=lax.Precision.HIGHEST)
    slot_rows = jnp.einsum(
        "mst,mtd->msd", token_select_b, inputs, preferred_element_type=jnp.float32
    ).astype(jnp.bfloat16)
    send_rows = jnp.repeat(slot_rows.reshape(n_micro, groups, CAP, feat_dim), hsplit, axis=1)
    send_weight = jnp.repeat(
        slot_weight.reshape(n_micro, groups, CAP).astype(jnp.bfloat16), hsplit, axis=1
    )
    recv_rows, recv_weight = in_one_piece((send_rows, send_weight), "expert", 1, 1, 3)
    expert_rows = recv_rows.reshape(n_micro, n_rows, feat_dim)
    expert_weight = recv_weight.reshape(n_micro, n_rows).astype(jnp.float32)
    w_gate = gate_weight[0]
    w_up = up_weight[0]
    w_down = down_weight[0]
    pre_gate = jnp.einsum("mrd,hd->mrh", expert_rows, w_gate, preferred_element_type=jnp.float32)
    pre_up = jnp.einsum("mrd,hd->mrh", expert_rows, w_up, preferred_element_type=jnp.float32)
    hidden = (pre_gate * jax.nn.sigmoid(pre_gate) * pre_up).astype(jnp.bfloat16)
    left_part = jnp.einsum(
        "mrh,hq->mrq", hidden, left_proj[0], preferred_element_type=jnp.float32
    ).astype(jnp.bfloat16)
    proj_right = right_proj[0]
    lag = n_section - 1 - section_id
    n_steps = n_section + n_micro - 1

    def one_step(step_num, loop_state):
        sending, grads_out, sketch = loop_state
        incoming = from_behind(sending, "section", -1)
        micro_idx = step_num - lag
        is_live = (micro_idx >= 0) & (micro_idx < n_micro)
        current = jnp.clip(micro_idx, 0, n_micro - 1)
        top_rows = lax.dynamic_index_in_dim(top_grad, current, 0, keepdims=False)
        out_grad = jnp.where(section_id == n_section - 1, top_rows, incoming)
        chosen = lax.dynamic_index_in_dim(token_select_b, current, 0, keepdims=False)
        grad_rows = jnp.dot(chosen, out_grad, preferred_element_type=jnp.float32).astype(
            jnp.bfloat16
        )
        spread_rows = jnp.repeat(grad_rows.reshape(groups, CAP, feat_dim), hsplit, axis=0)
        arrived = lax.all_to_all(spread_rows, "expert", split_axis=0, concat_axis=0, tiled=True)
        rows_weight = lax.dynamic_index_in_dim(expert_weight, current, 0, keepdims=False)
        gate_now = lax.dynamic_index_in_dim(pre_gate, current, 0, keepdims=False)
        up_now = lax.dynamic_index_in_dim(pre_up, current, 0, keepdims=False)
        left_now = lax.dynamic_index_in_dim(left_part, current, 0, keepdims=False)

        def backward(arrived_rows):
            grad_in = arrived_rows.reshape(n_rows, feat_dim)
            grad_hidden = (
                jnp.einsum("rd,hd->rh", grad_in, w_down, preferred_element_type=jnp.float32)
                * rows_weight[:, None]
            )
            sigmoid_g = jax.nn.sigmoid(gate_now)
            grad_gate = (
                grad_hidden * up_now * sigmoid_g * (1.0 + gate_now * (1.0 - sigmoid_g))
            ).astype(jnp.bfloat16)
            grad_up = (grad_hidden * gate_now * sigmoid_g).astype(jnp.bfloat16)
            part_grad = jnp.dot(grad_gate, w_gate, preferred_element_type=jnp.float32)
            part_grad = part_grad + jnp.dot(grad_up, w_up, preferred_element_type=jnp.float32)
            return part_grad.astype(jnp.bfloat16)

        part_grad = lax.cond(
            is_live,
            backward,
            lambda arrived_rows: jnp.zeros((n_rows, feat_dim), jnp.bfloat16),
            arrived,
        )
        back_part, back_left = sent_together(
            (
                part_grad.reshape(n_expert, CAP, feat_dim),
                left_now.reshape(n_expert, CAP, sketch_dim),
            ),
            "expert",
            0,
            0,
            2,
        )
        summed = back_part.reshape(groups, hsplit, CAP, feat_dim).astype(jnp.float32).sum(axis=1)
        summed = summed.reshape(n_slots, feat_dim)
        left_slots = (
            back_left.reshape(groups, hsplit, CAP, sketch_dim).astype(jnp.float32).sum(axis=1)
        )
        left_slots = left_slots.reshape(n_slots, sketch_dim)
        moe_grad = jnp.einsum(
            "st,sd->td", chosen.astype(jnp.float32), summed, precision=lax.Precision.HIGHEST
        )
        new_grad = (out_grad.astype(jnp.float32) + moe_grad).astype(jnp.bfloat16)
        right_tok = jnp.dot(out_grad, proj_right, preferred_element_type=jnp.float32)
        select_now = lax.dynamic_index_in_dim(select, current, 0, keepdims=False)
        weight_now = lax.dynamic_index_in_dim(weights_flat, current, 0, keepdims=False)
        ids_now = lax.dynamic_index_in_dim(ids_flat, current, 0, keepdims=False)
        example_now = lax.dynamic_index_in_dim(example_ids, current, 0, keepdims=False)
        left_pairs = jnp.einsum(
            "sp,sr->pr", select_now, left_slots, precision=lax.Precision.HIGHEST
        )
        right_pairs = jnp.repeat(right_tok, top_k, axis=0) * weight_now[:, None]
        example_pairs = jnp.repeat(example_now, top_k, axis=0)
        query = (current * EXM + example_pairs) * groups + ids_now
        query_hot = (query[:, None] == jnp.arange(q_total, dtype=jnp.int32)[None, :]).astype(
            jnp.float32
        )
        outer_rows = (query_hot[:, :, None] * left_pairs[:, None, :]).reshape(
            n_pairs, q_total * sketch_dim
        )
        contrib = jnp.einsum("pa,pb->ab", outer_rows, right_pairs, precision=lax.Precision.HIGHEST)
        sketch = sketch + jnp.where(
            is_live, contrib.reshape(q_total, sketch_dim * sketch_dim), jnp.float32(0.0)
        )
        updated = lax.dynamic_update_index_in_dim(grads_out, new_grad, current, 0)
        grads_out = jnp.where(is_live, updated, grads_out)
        return (new_grad, grads_out, sketch)

    start_state = (
        jnp.zeros((tok_dev, feat_dim), jnp.bfloat16),
        jnp.zeros((n_micro, tok_dev, feat_dim), jnp.bfloat16),
        jnp.zeros((q_total, sketch_dim * sketch_dim), jnp.float32),
    )
    final_state = lax.fori_loop(0, n_steps, one_step, start_state)
    sketch_share = sent_and_summed(final_state[2], "expert", 0)
    return (final_state[1][None], sketch_share[None])


def solution(mesh):
    placed = (
        P("section", None, "expert", None),
        P(None, "expert", None),
        P("section", None, "expert", None),
        P("section", None, "expert", None),
        P(None, "expert"),
        P("section", "expert", None),
        P("section", "expert", None),
        P("section", "expert", None),
        P("section", "expert", None),
        P("section", None, None),
    )
    return jax.shard_map(
        on_device,
        mesh=mesh,
        in_specs=placed,
        out_specs=(P("section", None, "expert", None), P("section", "expert", None)),
        check_vma=False,
    )
```

profile of v0, /device:TPU:6, one launch (start us, length us, event | category | flops | bytes accessed | tf_op | source)
XLA Modules:
  0.0 1114.7 jit_solution(2717566228579918237)
XLA Ops:
  7.0 13.5 %all-to-all-start.2 = ((bf16[2,32,3,2049]{3,0,2,1:T(2,128)(2,1)}), bf16[2,32,3,2049]{3,0,2,1:T(2,128)(2,1)S(1)}, u32[]{:S(2)}, u32[]{:S(2)}) async-start(bf16[2,32,3,2049]{3,0,2,1:T(2,128)(2,1)} %pad_maximum_fusion.1), calls=%async_computation.2 | async-start | bytes 1671168 | tf_op jit(solution)/shard_map/all_to_all | solution.py:15
  21.7 21.0 %all-to-all-done.2 = bf16[2,32,3,2049]{3,0,2,1:T(2,128)(2,1)S(1)} async-done(((bf16[2,32,3,2049]{3,0,2,1:T(2,128)(2,1)}), bf16[2,32,3,2049]{3,0,2,1:T(2,128)(2,1)S(1)}, u32[]{:S(2)}, u32[]{:S(2)}) %all-to-all-start.2) | async-done | bytes 786848 | tf_op jit(solution)/shard_map/all_to_all | solution.py:15
  51.7 1029.4 %while.20 = (s32[]{:T(128)}, bf16[8,2048]{1,0:T(8,128)(2,1)S(1)}, bf16[2,8,2048]{2,1,0:T(8,128)(2,1)S(1)}, f32[64,4096]{1,0:T(8,128)}, pred[]{:T(512)}, /*index=...) while((s32[]{:T(128)}, bf16[8,2048]{1,0:T(8,128)(2,1)S(1)}, ...), condition=%wide.region_8.9_spmd.clone, body=%wide.region_3.8_spmd.clone.sunk | while | flops 514401792 | bytes 25635464 | solution.py:212
  65.7 12.9 %all-to-all-done = bf16[32,3,2048]{2,1,0:T(4,128)(2,1)S(1)} async-done(((bf16[32,3,2048]{2,1,0:T(4,128)(2,1)}), bf16[32,3,2048]{2,1,0:T(4,128)(2,1)S(1)}, u32[]{:S(2)}, u32[]{:S(2)}) %all-to-all-start) | async-done | bytes 393248 | tf_op jit(solution)/shard_map/while/body/eval_jaxpr/all_to_all | solution.py:135
  90.3 14.6 %all-to-all-done.1 = bf16[32,3,2112]{2,1,0:T(4,128)(2,1)S(1)} async-done(((bf16[32,3,2112]{2,1,0:T(4,128)(2,1)}), bf16[32,3,2112]{2,1,0:T(4,128)(2,1)S(1)}, u32[]{:S(2)}, u32[]{:S(2)}) %all-to-all-start.1) | async-done | bytes 405536 | tf_op jit(solution)/shard_map/while/body/eval_jaxpr/all_to_all | solution.py:40
  124.6 12.3 %all-to-all-done = bf16[32,3,2048]{2,1,0:T(4,128)(2,1)S(1)} async-done(((bf16[32,3,2048]{2,1,0:T(4,128)(2,1)}), bf16[32,3,2048]{2,1,0:T(4,128)(2,1)S(1)}, u32[]{:S(2)}, u32[]{:S(2)}) %all-to-all-start) | async-done | bytes 393248 | tf_op jit(solution)/shard_map/while/body/eval_jaxpr/all_to_all | solution.py:135
  148.9 14.6 %all-to-all-done.1 = bf16[32,3,2112]{2,1,0:T(4,128)(2,1)S(1)} async-done(((bf16[32,3,2112]{2,1,0:T(4,128)(2,1)}), bf16[32,3,2112]{2,1,0:T(4,128)(2,1)S(1)}, u32[]{:S(2)}, u32[]{:S(2)}) %all-to-all-start.1) | async-done | bytes 405536 | tf_op jit(solution)/shard_map/while/body/eval_jaxpr/all_to_all | solution.py:40
  184.7 11.5 %all-to-all-done = bf16[32,3,2048]{2,1,0:T(4,128)(2,1)S(1)} async-done(((bf16[32,3,2048]{2,1,0:T(4,128)(2,1)}), bf16[32,3,2048]{2,1,0:T(4,128)(2,1)S(1)}, u32[]{:S(2)}, u32[]{:S(2)}) %all-to-all-start) | async-done | bytes 393248 | tf_op jit(solution)/shard_map/while/body/eval_jaxpr/all_to_all | solution.py:135
  209.0 14.8 %all-to-all-done.1 = bf16[32,3,2112]{2,1,0:T(4,128)(2,1)S(1)} async-done(((bf16[32,3,2112]{2,1,0:T(4,128)(2,1)}), bf16[32,3,2112]{2,1,0:T(4,128)(2,1)S(1)}, u32[]{:S(2)}, u32[]{:S(2)}) %all-to-all-start.1) | async-done | bytes 405536 | tf_op jit(solution)/shard_map/while/body/eval_jaxpr/all_to_all | solution.py:40
  268.9 15.0 %all-to-all-done.1 = bf16[32,3,2112]{2,1,0:T(4,128)(2,1)S(1)} async-done(((bf16[32,3,2112]{2,1,0:T(4,128)(2,1)}), bf16[32,3,2112]{2,1,0:T(4,128)(2,1)S(1)}, u32[]{:S(2)}, u32[]{:S(2)}) %all-to-all-start.1) | async-done | bytes 405536 | tf_op jit(solution)/shard_map/while/body/eval_jaxpr/all_to_all | solution.py:40
  305.0 11.2 %all-to-all-done = bf16[32,3,2048]{2,1,0:T(4,128)(2,1)S(1)} async-done(((bf16[32,3,2048]{2,1,0:T(4,128)(2,1)}), bf16[32,3,2048]{2,1,0:T(4,128)(2,1)S(1)}, u32[]{:S(2)}, u32[]{:S(2)}) %all-to-all-start) | async-done | bytes 393248 | tf_op jit(solution)/shard_map/while/body/eval_jaxpr/all_to_all | solution.py:135
  328.7 14.9 %all-to-all-done.1 = bf16[32,3,2112]{2,1,0:T(4,128)(2,1)S(1)} async-done(((bf16[32,3,2112]{2,1,0:T(4,128)(2,1)}), bf16[32,3,2112]{2,1,0:T(4,128)(2,1)S(1)}, u32[]{:S(2)}, u32[]{:S(2)}) %all-to-all-start.1) | async-done | bytes 405536 | tf_op jit(solution)/shard_map/while/body/eval_jaxpr/all_to_all | solution.py:40
  388.1 13.7 %all-to-all-done.1 = bf16[32,3,2112]{2,1,0:T(4,128)(2,1)S(1)} async-done(((bf16[32,3,2112]{2,1,0:T(4,128)(2,1)}), bf16[32,3,2112]{2,1,0:T(4,128)(2,1)S(1)}, u32[]{:S(2)}, u32[]{:S(2)}) %all-to-all-start.1) | async-done | bytes 405536 | tf_op jit(solution)/shard_map/while/body/eval_jaxpr/all_to_all | solution.py:40
  445.4 11.8 %all-to-all-done.1 = bf16[32,3,2112]{2,1,0:T(4,128)(2,1)S(1)} async-done(((bf16[32,3,2112]{2,1,0:T(4,128)(2,1)}), bf16[32,3,2112]{2,1,0:T(4,128)(2,1)S(1)}, u32[]{:S(2)}, u32[]{:S(2)}) %all-to-all-start.1) | async-done | bytes 405536 | tf_op jit(solution)/shard_map/while/body/eval_jaxpr/all_to_all | solution.py:40
  574.2 12.7 %collective-permute-done = bf16[8,2048]{1,0:T(8,128)(2,1)S(1)} collective-permute-done((bf16[8,2048]{1,0:T(8,128)(2,1)S(1)}, bf16[8,2048]{1,0:T(8,128)(2,1)S(1)}, u32[]{:S(2)}, u32[]{:S(2)}) %collective-permute-start) | collective-permute-done | bytes 32800 | tf_op jit(solution)/shard_map/while/body/eval_jaxpr/ppermute | solution.py:29
  634.9 12.6 %collective-permute-done = bf16[8,2048]{1,0:T(8,128)(2,1)S(1)} collective-permute-done((bf16[8,2048]{1,0:T(8,128)(2,1)S(1)}, bf16[8,2048]{1,0:T(8,128)(2,1)S(1)}, u32[]{:S(2)}, u32[]{:S(2)}) %collective-permute-start) | collective-permute-done | bytes 32800 | tf_op jit(solution)/shard_map/while/body/eval_jaxpr/ppermute | solution.py:29
  695.5 12.6 %collective-permute-done = bf16[8,2048]{1,0:T(8,128)(2,1)S(1)} collective-permute-done((bf16[8,2048]{1,0:T(8,128)(2,1)S(1)}, bf16[8,2048]{1,0:T(8,128)(2,1)S(1)}, u32[]{:S(2)}, u32[]{:S(2)}) %collective-permute-start) | collective-permute-done | bytes 32800 | tf_op jit(solution)/shard_map/while/body/eval_jaxpr/ppermute | solution.py:29
  756.0 12.6 %collective-permute-done = bf16[8,2048]{1,0:T(8,128)(2,1)S(1)} collective-permute-done((bf16[8,2048]{1,0:T(8,128)(2,1)S(1)}, bf16[8,2048]{1,0:T(8,128)(2,1)S(1)}, u32[]{:S(2)}, u32[]{:S(2)}) %collective-permute-start) | collective-permute-done | bytes 32800 | tf_op jit(solution)/shard_map/while/body/eval_jaxpr/ppermute | solution.py:29
  816.8 12.6 %collective-permute-done = bf16[8,2048]{1,0:T(8,128)(2,1)S(1)} collective-permute-done((bf16[8,2048]{1,0:T(8,128)(2,1)S(1)}, bf16[8,2048]{1,0:T(8,128)(2,1)S(1)}, u32[]{:S(2)}, u32[]{:S(2)}) %collective-permute-start) | collective-permute-done | bytes 32800 | tf_op jit(solution)/shard_map/while/body/eval_jaxpr/ppermute | solution.py:29
  864.5 15.0 %all-to-all-done.1 = bf16[32,3,2112]{2,1,0:T(4,128)(2,1)S(1)} async-done(((bf16[32,3,2112]{2,1,0:T(4,128)(2,1)}), bf16[32,3,2112]{2,1,0:T(4,128)(2,1)S(1)}, u32[]{:S(2)}, u32[]{:S(2)}) %all-to-all-start.1) | async-done | bytes 405536 | tf_op jit(solution)/shard_map/while/body/eval_jaxpr/all_to_all | solution.py:40
  937.6 20.2 %collective-permute-done = bf16[8,2048]{1,0:T(8,128)(2,1)S(1)} collective-permute-done((bf16[8,2048]{1,0:T(8,128)(2,1)S(1)}, bf16[8,2048]{1,0:T(8,128)(2,1)S(1)}, u32[]{:S(2)}, u32[]{:S(2)}) %collective-permute-start) | collective-permute-done | bytes 32800 | tf_op jit(solution)/shard_map/while/body/eval_jaxpr/ppermute | solution.py:29
  1012.9 11.2 %collective-permute-done = bf16[8,2048]{1,0:T(8,128)(2,1)S(1)} collective-permute-done((bf16[8,2048]{1,0:T(8,128)(2,1)S(1)}, bf16[8,2048]{1,0:T(8,128)(2,1)S(1)}, u32[]{:S(2)}, u32[]{:S(2)}) %collective-permute-start) | collective-permute-done | bytes 32800 | tf_op jit(solution)/shard_map/while/body/eval_jaxpr/ppermute | solution.py:29
  1062.8 11.8 %all-to-all-done.1 = bf16[32,3,2112]{2,1,0:T(4,128)(2,1)S(1)} async-done(((bf16[32,3,2112]{2,1,0:T(4,128)(2,1)}), bf16[32,3,2112]{2,1,0:T(4,128)(2,1)S(1)}, u32[]{:S(2)}, u32[]{:S(2)}) %all-to-all-start.1) | async-done | bytes 405536 | tf_op jit(solution)/shard_map/while/body/eval_jaxpr/all_to_all | solution.py:40
  1083.0 30.7 %all_to_all.36 = f32[32,2,4096]{2,1,0:T(2,128)S(1)} all-to-all(f32[32,2,4096]{2,1,0:T(2,128)S(1)} %reshape.253), channel_id=1, replica_groups=mesh['section'=16,'expert'=32] {'expert'}, dimensions={0} | all-to-all | bytes 2097152 | tf_op jit(solution)/shard_map/all_to_all | solution.py:54
  (888 shorter events, 794.1 us)
Async XLA Ops:
  7.0 35.6 %all-to-all-start.2 = ((bf16[2,32,3,2049]{3,0,2,1:T(2,128)(2,1)}), bf16[2,32,3,2049]{3,0,2,1:T(2,128)(2,1)S(1)}, u32[]{:S(2)}, u32[]{:S(2)}) async-start(bf16[2,32,3,2049]{3,0,2,1:T(2,128)(2,1)} %pad_maximum_fusion.1), calls=%async_computation.2 | async-start | bytes 1671168 | tf_op jit(solution)/shard_map/all_to_all | solution.py:15
  56.9 21.7 %all-to-all-start = ((bf16[32,3,2048]{2,1,0:T(4,128)(2,1)}), bf16[32,3,2048]{2,1,0:T(4,128)(2,1)S(1)}, u32[]{:S(2)}, u32[]{:S(2)}) async-start(bf16[32,3,2048]{2,1,0:T(4,128)(2,1)} %bitcast.153), calls=%async_computation | async-start | bytes 1048576 | tf_op jit(solution)/shard_map/while/body/eval_jaxpr/all_to_all | solution.py:135
  79.9 24.9 %all-to-all-start.1 = ((bf16[32,3,2112]{2,1,0:T(4,128)(2,1)}), bf16[32,3,2112]{2,1,0:T(4,128)(2,1)S(1)}, u32[]{:S(2)}, u32[]{:S(2)}) async-start(bf16[32,3,2112]{2,1,0:T(4,128)(2,1)} %pad_maximum_fusion.3), calls=%async_computation.1 | async-start | bytes 1114112 | tf_op jit(solution)/shard_map/while/body/eval_jaxpr/all_to_all | solution.py:40
  115.4 21.5 %all-to-all-start = ((bf16[32,3,2048]{2,1,0:T(4,128)(2,1)}), bf16[32,3,2048]{2,1,0:T(4,128)(2,1)S(1)}, u32[]{:S(2)}, u32[]{:S(2)}) async-start(bf16[32,3,2048]{2,1,0:T(4,128)(2,1)} %bitcast.153), calls=%async_computation | async-start | bytes 1048576 | tf_op jit(solution)/shard_map/while/body/eval_jaxpr/all_to_all | solution.py:135
  138.2 25.3 %all-to-all-start.1 = ((bf16[32,3,2112]{2,1,0:T(4,128)(2,1)}), bf16[32,3,2112]{2,1,0:T(4,128)(2,1)S(1)}, u32[]{:S(2)}, u32[]{:S(2)}) async-start(bf16[32,3,2112]{2,1,0:T(4,128)(2,1)} %pad_maximum_fusion.3), calls=%async_computation.1 | async-start | bytes 1114112 | tf_op jit(solution)/shard_map/while/body/eval_jaxpr/all_to_all | solution.py:40
  175.2 20.9 %all-to-all-start = ((bf16[32,3,2048]{2,1,0:T(4,128)(2,1)}), bf16[32,3,2048]{2,1,0:T(4,128)(2,1)S(1)}, u32[]{:S(2)}, u32[]{:S(2)}) async-start(bf16[32,3,2048]{2,1,0:T(4,128)(2,1)} %bitcast.153), calls=%async_computation | async-start | bytes 1048576 | tf_op jit(solution)/shard_map/while/body/eval_jaxpr/all_to_all | solution.py:135
  197.5 26.2 %all-to-all-start.1 = ((bf16[32,3,2112]{2,1,0:T(4,128)(2,1)}), bf16[32,3,2112]{2,1,0:T(4,128)(2,1)S(1)}, u32[]{:S(2)}, u32[]{:S(2)}) async-start(bf16[32,3,2112]{2,1,0:T(4,128)(2,1)} %pad_maximum_fusion.3), calls=%async_computation.1 | async-start | bytes 1114112 | tf_op jit(solution)/shard_map/while/body/eval_jaxpr/all_to_all | solution.py:40
  235.5 20.6 %all-to-all-start = ((bf16[32,3,2048]{2,1,0:T(4,128)(2,1)}), bf16[32,3,2048]{2,1,0:T(4,128)(2,1)S(1)}, u32[]{:S(2)}, u32[]{:S(2)}) async-start(bf16[32,3,2048]{2,1,0:T(4,128)(2,1)} %bitcast.153), calls=%async_computation | async-start | bytes 1048576 | tf_op jit(solution)/shard_map/while/body/eval_jaxpr/all_to_all | solution.py:135
  257.4 26.4 %all-to-all-start.1 = ((bf16[32,3,2112]{2,1,0:T(4,128)(2,1)}), bf16[32,3,2112]{2,1,0:T(4,128)(2,1)S(1)}, u32[]{:S(2)}, u32[]{:S(2)}) async-start(bf16[32,3,2112]{2,1,0:T(4,128)(2,1)} %pad_maximum_fusion.3), calls=%async_computation.1 | async-start | bytes 1114112 | tf_op jit(solution)/shard_map/while/body/eval_jaxpr/all_to_all | solution.py:40
  295.6 20.7 %all-to-all-start = ((bf16[32,3,2048]{2,1,0:T(4,128)(2,1)}), bf16[32,3,2048]{2,1,0:T(4,128)(2,1)S(1)}, u32[]{:S(2)}, u32[]{:S(2)}) async-start(bf16[32,3,2048]{2,1,0:T(4,128)(2,1)} %bitcast.153), calls=%async_computation | async-start | bytes 1048576 | tf_op jit(solution)/shard_map/while/body/eval_jaxpr/all_to_all | solution.py:135
  317.6 26.0 %all-to-all-start.1 = ((bf16[32,3,2112]{2,1,0:T(4,128)(2,1)}), bf16[32,3,2112]{2,1,0:T(4,128)(2,1)S(1)}, u32[]{:S(2)}, u32[]{:S(2)}) async-start(bf16[32,3,2112]{2,1,0:T(4,128)(2,1)} %pad_maximum_fusion.3), calls=%async_computation.1 | async-start | bytes 1114112 | tf_op jit(solution)/shard_map/while/body/eval_jaxpr/all_to_all | solution.py:40
  355.3 20.5 %all-to-all-start = ((bf16[32,3,2048]{2,1,0:T(4,128)(2,1)}), bf16[32,3,2048]{2,1,0:T(4,128)(2,1)S(1)}, u32[]{:S(2)}, u32[]{:S(2)}) async-start(bf16[32,3,2048]{2,1,0:T(4,128)(2,1)} %bitcast.153), calls=%async_computation | async-start | bytes 1048576 | tf_op jit(solution)/shard_map/while/body/eval_jaxpr/all_to_all | solution.py:135
  377.1 24.7 %all-to-all-start.1 = ((bf16[32,3,2112]{2,1,0:T(4,128)(2,1)}), bf16[32,3,2112]{2,1,0:T(4,128)(2,1)S(1)}, u32[]{:S(2)}, u32[]{:S(2)}) async-start(bf16[32,3,2112]{2,1,0:T(4,128)(2,1)} %pad_maximum_fusion.3), calls=%async_computation.1 | async-start | bytes 1114112 | tf_op jit(solution)/shard_map/while/body/eval_jaxpr/all_to_all | solution.py:40
  414.6 19.3 %all-to-all-start = ((bf16[32,3,2048]{2,1,0:T(4,128)(2,1)}), bf16[32,3,2048]{2,1,0:T(4,128)(2,1)S(1)}, u32[]{:S(2)}, u32[]{:S(2)}) async-start(bf16[32,3,2048]{2,1,0:T(4,128)(2,1)} %bitcast.153), calls=%async_computation | async-start | bytes 1048576 | tf_op jit(solution)/shard_map/while/body/eval_jaxpr/all_to_all | solution.py:135
  435.2 22.0 %all-to-all-start.1 = ((bf16[32,3,2112]{2,1,0:T(4,128)(2,1)}), bf16[32,3,2112]{2,1,0:T(4,128)(2,1)S(1)}, u32[]{:S(2)}, u32[]{:S(2)}) async-start(bf16[32,3,2112]{2,1,0:T(4,128)(2,1)} %pad_maximum_fusion.3), calls=%async_computation.1 | async-start | bytes 1114112 | tf_op jit(solution)/shard_map/while/body/eval_jaxpr/all_to_all | solution.py:40
  491.7 18.9 %all-to-all-start.1 = ((bf16[32,3,2112]{2,1,0:T(4,128)(2,1)}), bf16[32,3,2112]{2,1,0:T(4,128)(2,1)S(1)}, u32[]{:S(2)}, u32[]{:S(2)}) async-start(bf16[32,3,2112]{2,1,0:T(4,128)(2,1)} %pad_maximum_fusion.3), calls=%async_computation.1 | async-start | bytes 1114112 | tf_op jit(solution)/shard_map/while/body/eval_jaxpr/all_to_all | solution.py:40
  547.5 18.8 %all-to-all-start.1 = ((bf16[32,3,2112]{2,1,0:T(4,128)(2,1)}), bf16[32,3,2112]{2,1,0:T(4,128)(2,1)S(1)}, u32[]{:S(2)}, u32[]{:S(2)}) async-start(bf16[32,3,2112]{2,1,0:T(4,128)(2,1)} %pad_maximum_fusion.3), calls=%async_computation.1 | async-start | bytes 1114112 | tf_op jit(solution)/shard_map/while/body/eval_jaxpr/all_to_all | solution.py:40
  790.1 18.8 %all-to-all-start.1 = ((bf16[32,3,2112]{2,1,0:T(4,128)(2,1)}), bf16[32,3,2112]{2,1,0:T(4,128)(2,1)S(1)}, u32[]{:S(2)}, u32[]{:S(2)}) async-start(bf16[32,3,2112]{2,1,0:T(4,128)(2,1)} %pad_maximum_fusion.3), calls=%async_computation.1 | async-start | bytes 1114112 | tf_op jit(solution)/shard_map/while/body/eval_jaxpr/all_to_all | solution.py:40
  831.5 20.2 %all-to-all-start = ((bf16[32,3,2048]{2,1,0:T(4,128)(2,1)}), bf16[32,3,2048]{2,1,0:T(4,128)(2,1)S(1)}, u32[]{:S(2)}, u32[]{:S(2)}) async-start(bf16[32,3,2048]{2,1,0:T(4,128)(2,1)} %bitcast.153), calls=%async_computation | async-start | bytes 1048576 | tf_op jit(solution)/shard_map/while/body/eval_jaxpr/all_to_all | solution.py:135
  853.0 26.4 %all-to-all-start.1 = ((bf16[32,3,2112]{2,1,0:T(4,128)(2,1)}), bf16[32,3,2112]{2,1,0:T(4,128)(2,1)S(1)}, u32[]{:S(2)}, u32[]{:S(2)}) async-start(bf16[32,3,2112]{2,1,0:T(4,128)(2,1)} %pad_maximum_fusion.3), calls=%async_computation.1 | async-start | bytes 1114112 | tf_op jit(solution)/shard_map/while/body/eval_jaxpr/all_to_all | solution.py:40
  911.0 18.7 %all-to-all-start.1 = ((bf16[32,3,2112]{2,1,0:T(4,128)(2,1)}), bf16[32,3,2112]{2,1,0:T(4,128)(2,1)S(1)}, u32[]{:S(2)}, u32[]{:S(2)}) async-start(bf16[32,3,2112]{2,1,0:T(4,128)(2,1)} %pad_maximum_fusion.3), calls=%async_computation.1 | async-start | bytes 1114112 | tf_op jit(solution)/shard_map/while/body/eval_jaxpr/all_to_all | solution.py:40
  936.2 21.5 %collective-permute-start = (bf16[8,2048]{1,0:T(8,128)(2,1)S(1)}, bf16[8,2048]{1,0:T(8,128)(2,1)S(1)}, u32[]{:S(2)}, u32[]{:S(2)}) collective-permute-start(bf16[8,2048]{1,0:T(8,128)(2,1)S(1)} %broadcast_select_fusion.2), channel_id=1, source_target_pairs={{32,0},{64,32},{96,64},{128,96},{160,128},{192,160},{224,192},{256... | collective-permute-start | bytes 98312 | tf_op jit(solution)/shard_map/while/body/eval_jaxpr/ppermute | solution.py:29
  986.3 18.8 %all-to-all-start.1 = ((bf16[32,3,2112]{2,1,0:T(4,128)(2,1)}), bf16[32,3,2112]{2,1,0:T(4,128)(2,1)S(1)}, u32[]{:S(2)}, u32[]{:S(2)}) async-start(bf16[32,3,2112]{2,1,0:T(4,128)(2,1)} %pad_maximum_fusion.3), calls=%async_computation.1 | async-start | bytes 1114112 | tf_op jit(solution)/shard_map/while/body/eval_jaxpr/all_to_all | solution.py:40
  1052.7 21.9 %all-to-all-start.1 = ((bf16[32,3,2112]{2,1,0:T(4,128)(2,1)}), bf16[32,3,2112]{2,1,0:T(4,128)(2,1)S(1)}, u32[]{:S(2)}, u32[]{:S(2)}) async-start(bf16[32,3,2112]{2,1,0:T(4,128)(2,1)} %pad_maximum_fusion.3), calls=%async_computation.1 | async-start | bytes 1114112 | tf_op jit(solution)/shard_map/while/body/eval_jaxpr/all_to_all | solution.py:40
  (134 other events, 2404.1 us)
where the time goes:
time: 1130 us; the launch traced here: 1110 us
  waiting for transfers between devices  520 us (46%)
  starting transfers between devices  306 us (27%)
  other arithmetic  96.1 us (9%)
  matrix products  78.9 us (7%)
  local copies, waits for them, and re-layouts  78.3 us (7%)
  blocking collectives  30.7 us (3%)
    all_to_all x17, waiting for transfers between devices, sent_together(): lax.all_to_all(both, axis, split_axis=split_dim, concat_axis=concat_dim,...  204 us
    all_to_all x17, waiting for transfers between devices, one_step(): lax.all_to_all(spread_rows, 'expert', split_axis=0, concat_axis=0, tiled=...  172 us
    all_to_all x17, starting transfers between devices, sent_together(): lax.all_to_all(both, axis, split_axis=split_dim, concat_axis=concat_dim,...  144 us
    all_to_all x17, starting transfers between devices, one_step(): lax.all_to_all(spread_rows, 'expert', split_axis=0, concat_axis=0, tiled=...  126 us
    ppermute x17, waiting for transfers between devices, from_behind(): return lax.ppermute(block, axis, route)  123 us
    add x17, other arithmetic, one_step(): sketch + jnp.where(is_live, contrib.reshape(q_total, sketch_dim * sketch_...  38.3 us
    all_to_all x1, blocking collectives, sent_and_summed(): lax.all_to_all(blocks, axis, split_axis=0, concat_axis=0, tiled=True)  30.7 us
  transfers between devices with their start and end apart: 52, of which 52 were waited for; matrix products, arithmetic and copies ran while one was open for 5% of the time, Pallas kernels for 0%

commit v1 on v0

v1 whole, which is shorter than its diff:
```python
import functools

import jax
import jax.numpy as jnp
from jax import lax
from jax.experimental import pallas as pl
from jax.experimental.pallas import tpu as pltpu
from jax.sharding import PartitionSpec as P

EXPERTS = 8
EXM = 4
CAP = 3
LANES = 128
F32 = jnp.float32
BF16 = jnp.bfloat16
MESH = pl.DeviceIdType.MESH


def kernel(
    n_section,
    n_expert,
    groups,
    tok_ref,
    row_ref,
    x_ref,
    top_ref,
    meta_ref,
    left_ref,
    gate_hbm,
    up_hbm,
    down_hbm,
    right_hbm,
    grads_ref,
    sketch_ref,
    wgu,
    wdr,
    xsend,
    xrecv,
    gsend,
    grecv,
    osend,
    crecv_a,
    crecv_b,
    frecv_a,
    frecv_b,
    metar,
    outgrad,
    resid,
    back,
    wide,
    rows,
    gcat,
    coef_g,
    coef_u,
    left_keep,
    psend,
    srecv,
    w_sem,
    xs_sem,
    xr_sem,
    gs_sem,
    gr_sem,
    os_sem,
    cr_sem,
    fr_sem,
    ms_sem,
    mr_sem,
    rs_sem,
    rr_sem,
    bs_sem,
    br_sem,
    ss_sem,
    sr_sem,
):
    crecv, frecv = (crecv_a, crecv_b), (frecv_a, frecv_b)
    sec = lax.axis_index("section")
    me = lax.axis_index("expert")
    hsplit = n_expert // groups
    n_micro, tok_dev = top_ref.shape[:2]
    n_slots = groups * CAP
    dk = x_ref.shape[1]
    hid = down_hbm.shape[0]
    top_k = row_ref.shape[0] // (n_micro * tok_dev)
    q_dev = n_micro * EXM * groups // n_expert
    r_dim = left_ref.shape[0]
    half = r_dim // 2
    last = sec == n_section - 1
    first = sec == 0

    loads = [
        pltpu.make_async_copy(gate_hbm, wgu.at[pl.ds(0, hid)], w_sem.at[0]),
        pltpu.make_async_copy(up_hbm, wgu.at[pl.ds(hid, hid)], w_sem.at[1]),
        pltpu.make_async_copy(down_hbm, wdr.at[pl.ds(0, hid)], w_sem.at[2]),
        pltpu.make_async_copy(right_hbm, wdr.at[pl.ds(hid, r_dim)], w_sem.at[3]),
    ]
    for load in loads:
        load.start()

    barrier = pltpu.get_barrier_semaphore()

    def greet(other, skip_me):
        def one(n, carry):
            to = lax.rem(me + 1 + n, n_expert)
            pl.semaphore_signal(
                barrier, inc=1, device_id={"section": other, "expert": to}, device_id_type=MESH
            )
            return carry

        lax.fori_loop(0, n_expert - 1 if skip_me else n_expert, one, 0)

    greet(sec, True)

    @pl.when(jnp.logical_not(first))
    def _():
        greet(sec - 1, False)

    @pl.when(jnp.logical_not(last))
    def _():
        greet(sec + 1, False)

    def xbuild(m, carry):
        for s in range(n_slots):
            xsend[m, s] = x_ref[m * tok_dev + tok_ref[m * n_slots + s]]
        return carry

    lax.fori_loop(0, n_micro, xbuild, 0)

    met = (
        n_expert - 1
        + jnp.where(first, 0, n_expert)
        + jnp.where(last, 0, n_expert)
    )
    pl.semaphore_wait(barrier, met)

    def spread(src, per, dst, send_sem, recv_sem):
        def one(n, carry):
            to = lax.rem(me + 1 + n, n_expert)
            pltpu.make_async_remote_copy(
                src_ref=src.at[pl.ds((to // hsplit) * per, per)],
                dst_ref=dst.at[pl.ds(me * per, per)],
                send_sem=send_sem,
                recv_sem=recv_sem,
                device_id={"section": sec, "expert": to},
                device_id_type=MESH,
            ).start()
            return carry

        lax.fori_loop(0, n_expert - 1, one, 0)
        pltpu.make_async_copy(
            src.at[pl.ds((me // hsplit) * per, per)], dst.at[pl.ds(me * per, per)], recv_sem
        ).start()

    def await_all(ref, sem):
        pltpu.make_async_copy(ref, ref, sem).wait()

    def dispatch(m):
        for s in range(n_slots):
            gsend[m, s] = outgrad[m, tok_ref[m * n_slots + s]]
        spread(gsend.at[m], CAP, grecv.at[m], gs_sem.at[m], gr_sem.at[m])

        @pl.when(jnp.logical_not(first))
        def _():
            pltpu.make_async_remote_copy(
                src_ref=outgrad.at[m],
                dst_ref=resid.at[m],
                send_sem=rs_sem.at[m],
                recv_sem=rr_sem.at[m],
                device_id={"section": sec - 1, "expert": me},
                device_id_type=MESH,
            ).start()

        @pl.when(jnp.logical_not(last))
        def _():
            pltpu.make_async_remote_copy(
                src_ref=outgrad.at[m],
                dst_ref=back.at[m],
                send_sem=bs_sem.at[m],
                recv_sem=br_sem.at[m],
                device_id={"section": sec + 1, "expert": me},
                device_id_type=MESH,
            ).start()

    def combined(m, t, base, parts, which):
        total = base
        for k in range(top_k):
            at = row_ref[m * tok_dev * top_k + t * top_k + k, which]
            for j in range(hsplit):
                total = total + parts[at + j * CAP].astype(F32)
        return total

    def start_micro(m, carry):
        spread(xsend.at[m], CAP, xrecv.at[m], xs_sem.at[m], xr_sem.at[m])

        @pl.when(m == 0)
        def _():
            spread(meta_ref, 16, metar, ms_sem, mr_sem)

        @pl.when(last)
        def _():
            outgrad[m] = top_ref[m]
            dispatch(m)

        return carry

    lax.fori_loop(0, n_micro, start_micro, 0)

    def by_row(ref, m):
        wide[...] = ref[m].reshape(n_expert * CAP * dk, LANES).astype(F32)
        for k in range(dk):
            for c in range(CAP):
                rows[pl.ds(c * n_expert, n_expert), pl.ds(k * LANES, LANES)] = wide[
                    pl.ds(c * dk + k, n_expert, stride=CAP * dk), :
                ].astype(BF16)

    def meta_of(m):
        return jnp.concatenate(
            [
                jnp.concatenate(
                    [metar[pl.ds(b * 8 + m * 4 + c, n_expert, stride=16), :] for b in range(2)],
                    axis=1,
                )
                for c in range(CAP)
            ],
            axis=0,
        )

    contract_last = (((1,), (1,)), ((), ()))
    for load in loads:
        load.wait()
    await_all(metar, mr_sem)

    def forward(m, carry):
        await_all(xrecv.at[m], xr_sem.at[m])
        by_row(xrecv, m)
        both = lax.dot_general(rows[...], wgu[...], contract_last, preferred_element_type=F32)
        pre_gate, pre_up = both[:, :hid], both[:, hid:]
        sigmoid_g = jax.nn.sigmoid(pre_gate)
        silu = pre_gate * sigmoid_g
        hidden = (silu * pre_up).astype(BF16)
        left_keep[m] = lax.dot_general(
            hidden, left_ref[...], contract_last, preferred_element_type=F32
        )
        weight = jnp.max(meta_of(m), axis=1, keepdims=True)
        coef_g[m] = weight * (pre_up * sigmoid_g * (1.0 + pre_gate * (1.0 - sigmoid_g)))
        coef_u[m] = weight * silu
        return carry

    lax.fori_loop(0, n_micro, forward, 0)

    def to_homes(m, other, skip_me, dst, recv_sem):
        def one(n, carry):
            to = lax.rem(me + 1 + n, n_expert)
            pltpu.make_async_remote_copy(
                src_ref=osend.at[m, pl.ds(to * CAP, CAP)],
                dst_ref=dst.at[pl.ds(me * CAP, CAP)],
                send_sem=os_sem.at[m],
                recv_sem=recv_sem,
                device_id={"section": other, "expert": to},
                device_id_type=MESH,
            ).start()
            return carry

        lax.fori_loop(0, n_expert - 1 if skip_me else n_expert, one, 0)

    def sketch_copies(m):
        mine = me // hsplit
        copies = []
        for ex in range(EXM):
            q = (m * EXM + ex) * groups + mine
            to = q // q_dev
            src = psend.at[m, ex]
            dst = srecv.at[lax.rem(q, q_dev), lax.rem(me, hsplit)]
            far = pltpu.make_async_remote_copy(
                src_ref=src,
                dst_ref=dst,
                send_sem=ss_sem.at[m, ex],
                recv_sem=sr_sem,
                device_id={"section": sec, "expert": to},
                device_id_type=MESH,
            )
            near = pltpu.make_async_copy(src, dst, sr_sem)
            copies.append((to, far, near))
        return copies

    def step(m, carry):
        @pl.when(jnp.logical_not(last))
        def _():
            await_all(resid.at[m], rr_sem.at[m])
            for which in range(n_micro):

                @pl.when(m == which)
                def _():
                    await_all(crecv[which], cr_sem.at[which])
                    for t in range(tok_dev):
                        base = resid[which, t].astype(F32)
                        total = combined(which, t, base, crecv[which], 0)
                        outgrad[which, t] = total.astype(BF16)

            dispatch(m)

        await_all(grecv.at[m], gr_sem.at[m])
        by_row(grecv, m)
        both = lax.dot_general(
            rows[...], wdr[...], contract_last, preferred_element_type=F32
        )
        grad_hidden, right = both[:, :hid], both[:, hid:]
        gcat[:, pl.ds(0, hid)] = (grad_hidden * coef_g[m]).astype(BF16)
        gcat[:, pl.ds(hid, hid)] = (grad_hidden * coef_u[m]).astype(BF16)
        for n in range(dk // 2):
            part = jnp.dot(
                gcat[...], wgu[:, pl.ds(n * 2 * LANES, 2 * LANES)], preferred_element_type=F32
            )
            for b in range(2):
                k = n * 2 + b
                for c in range(CAP):
                    wide[pl.ds(c * dk + k, n_expert, stride=CAP * dk), :] = part[
                        c * n_expert : (c + 1) * n_expert, b * LANES : (b + 1) * LANES
                    ]
        osend[m] = wide[...].astype(BF16).reshape(n_expert * CAP, dk, LANES)

        for which in range(n_micro):

            @pl.when((m == which) & first)
            def _():
                to_homes(which, sec, True, frecv[which], fr_sem.at[which])
                pltpu.make_async_copy(
                    osend.at[which, pl.ds(me * CAP, CAP)],
                    frecv[which].at[pl.ds(me * CAP, CAP)],
                    fr_sem.at[which],
                ).start()

            @pl.when((m == which) & jnp.logical_not(first))
            def _():
                to_homes(which, sec - 1, False, crecv[which], cr_sem.at[which])

        right = jnp.concatenate([right] * EXM, axis=1) * meta_of(m)
        left = left_keep[m].astype(BF16)
        at_r = lax.broadcasted_iota(jnp.int32, (r_dim, r_dim), 0)
        at_c = lax.broadcasted_iota(jnp.int32, (r_dim, r_dim), 1)
        place = lax.rem(at_r, 2) * half + lax.div(at_r, 2)
        shuffle = jnp.where(at_c == place, 1.0, 0.0).astype(BF16)
        left = jnp.dot(left, shuffle, preferred_element_type=F32).astype(BF16)
        outer = lax.dot_general(
            left, right.astype(BF16), (((0,), (0,)), ((), ())), preferred_element_type=F32
        )
        for ex in range(EXM):
            block = outer[:, ex * r_dim : (ex + 1) * r_dim]
            psend[m, ex] = jnp.concatenate([block[:half], block[half:]], axis=1)
        for to, far, near in sketch_copies(m):

            @pl.when(to != me)
            def _():
                far.start()

            @pl.when(to == me)
            def _():
                near.start()

        return carry

    lax.fori_loop(0, n_micro, step, 0)

    @pl.when(first)
    def _():
        for m in range(n_micro):
            await_all(frecv[m], fr_sem.at[m])
            for t in range(tok_dev):
                total = combined(m, t, outgrad[m, t].astype(F32), frecv[m], 1)
                grads_ref[m, t] = total.astype(BF16)

    @pl.when(jnp.logical_not(first))
    def _():
        for m in range(n_micro):
            await_all(back.at[m], br_sem.at[m])
        grads_ref[...] = back[...]

    await_all(srecv, sr_sem)
    for q in range(q_dev):
        total = srecv[q, 0]
        for j in range(1, hsplit):
            total = total + srecv[q, j]
        sketch_ref[q] = total

    others = (n_expert - 1) * CAP
    await_all(metar.at[pl.ds(0, (n_expert - 1) * 16)], ms_sem)
    for m in range(n_micro):
        await_all(xrecv.at[m, pl.ds(0, others)], xs_sem.at[m])
        await_all(grecv.at[m, pl.ds(0, others)], gs_sem.at[m])

        @pl.when(first)
        def _():
            await_all(osend.at[m, pl.ds(0, others)], os_sem.at[m])

        @pl.when(jnp.logical_not(first))
        def _():
            await_all(osend.at[m], os_sem.at[m])
            await_all(outgrad.at[m], rs_sem.at[m])

        @pl.when(jnp.logical_not(last))
        def _():
            await_all(outgrad.at[m], bs_sem.at[m])

        for to, far, near in sketch_copies(m):

            @pl.when(to != me)
            def _():
                far.wait_send()


def on_device(
    saved_inputs,
    top_grad,
    expert_ids,
    route_weights,
    example_ids,
    gate_weight,
    up_weight,
    down_weight,
    left_proj,
    right_proj,
):
    n_section = lax.axis_size("section")
    n_expert = lax.axis_size("expert")
    groups = EXPERTS
    hsplit = n_expert // groups
    n_micro, tok_dev, feat = saved_inputs.shape[1:]
    top_k = expert_ids.shape[3]
    n_pairs = tok_dev * top_k
    n_slots = groups * CAP
    dk = feat // LANES
    hid = gate_weight.shape[1]
    r_dim = left_proj.shape[2]
    q_dev = n_micro * EXM * groups // n_expert

    ids = expert_ids[0].reshape(n_micro, n_pairs)
    weights = route_weights[0].reshape(n_micro, n_pairs).astype(F32)
    pair = jnp.arange(n_pairs, dtype=jnp.int32)
    same = (ids[:, :, None] == ids[:, None, :]) & (pair[:, None] > pair[None, :])[None]
    position = jnp.sum(same.astype(jnp.int32), axis=2)
    slot_of = ids * CAP + position
    row_of = ids * (hsplit * CAP) + position
    slots = jnp.arange(n_slots, dtype=jnp.int32)
    select = slot_of[:, None, :] == slots[None, :, None]
    tok_of_slot = jnp.sum(jnp.where(select, (pair // top_k)[None, None], 0), axis=2)
    slot_weight = jnp.sum(jnp.where(select, weights[:, None, :], 0.0), axis=2)
    example_pairs = jnp.repeat(example_ids, top_k, axis=1)
    slot_example = jnp.sum(jnp.where(select, example_pairs[:, None, :], 0), axis=2)
    lane_example = jnp.arange(EXM * r_dim, dtype=jnp.int32) // r_dim
    meta = jnp.where(
        slot_example[:, :, None] == lane_example[None, None], slot_weight[:, :, None], 0.0
    )
    meta = meta.reshape(n_micro, groups, CAP, EXM * r_dim).swapaxes(0, 1)
    meta = jnp.pad(meta, ((0, 0), (0, 0), (0, 4 - CAP), (0, 0)))
    meta = meta.reshape(groups, n_micro * 4, 2, LANES).swapaxes(1, 2)
    meta = meta.reshape(groups * 2 * n_micro * 4, LANES)
    row_flat = row_of.reshape(n_micro * n_pairs)
    above = lax.ppermute(row_flat, "section", [(i, i - 1) for i in range(1, n_section)])
    row_table = jnp.stack([above, row_flat], axis=1)

    n_rows = n_expert * CAP
    vmem = pl.BlockSpec(memory_space=pltpu.VMEM)
    smem = pl.BlockSpec(memory_space=pltpu.SMEM)
    hbm = pl.BlockSpec(memory_space=pl.ANY)
    dma = pltpu.SemaphoreType.DMA
    grads, sketch = pl.pallas_call(
        functools.partial(kernel, n_section, n_expert, groups),
        out_shape=(
            jax.ShapeDtypeStruct((n_micro, tok_dev, dk, LANES), BF16),
            jax.ShapeDtypeStruct((q_dev, r_dim // 2, 2 * r_dim), F32),
        ),
        in_specs=[smem, smem, vmem, vmem, vmem, vmem, hbm, hbm, hbm, hbm],
        out_specs=(vmem, vmem),
        scratch_shapes=[
            pltpu.VMEM((2 * hid, feat), BF16),
            pltpu.VMEM((hid + r_dim, feat), BF16),
            pltpu.VMEM((n_micro, n_slots, dk, LANES), BF16),
            pltpu.VMEM((n_micro, n_rows, dk, LANES), BF16),
            pltpu.VMEM((n_micro, n_slots, dk, LANES), BF16),
            pltpu.VMEM((n_micro, n_rows, dk, LANES), BF16),
            pltpu.VMEM((n_micro, n_rows, dk, LANES), BF16),
            pltpu.VMEM((n_rows, dk, LANES), BF16),
            pltpu.VMEM((n_rows, dk, LANES), BF16),
            pltpu.VMEM((n_rows, dk, LANES), BF16),
            pltpu.VMEM((n_rows, dk, LANES), BF16),
            pltpu.VMEM((n_expert * 16, LANES), F32),
            pltpu.VMEM((n_micro, tok_dev, dk, LANES), BF16),
            pltpu.VMEM((n_micro, tok_dev, dk, LANES), BF16),
            pltpu.VMEM((n_micro, tok_dev, dk, LANES), BF16),
            pltpu.VMEM((n_rows * dk, LANES), F32),
            pltpu.VMEM((n_rows, feat), BF16),
            pltpu.VMEM((n_rows, 2 * hid), BF16),
            pltpu.VMEM((n_micro, n_rows, hid), F32),
            pltpu.VMEM((n_micro, n_rows, hid), F32),
            pltpu.VMEM((n_micro, n_rows, r_dim), F32),
            pltpu.VMEM((n_micro, EXM, r_dim // 2, 2 * r_dim), F32),
            pltpu.VMEM((q_dev, hsplit, r_dim // 2, 2 * r_dim), F32),
            dma((4,)),
            dma((n_micro,)),
            dma((n_micro,)),
            dma((n_micro,)),
            dma((n_micro,)),
            dma((n_micro,)),
            dma((n_micro,)),
            dma((n_micro,)),
            dma(()),
            dma(()),
            dma((n_micro,)),
            dma((n_micro,)),
            dma((n_micro,)),
            dma((n_micro,)),
            dma((n_micro, EXM)),
            dma(()),
        ],
        compiler_params=pltpu.CompilerParams(collective_id=0, has_side_effects=True),
    )(
        tok_of_slot.reshape(n_micro * n_slots),
        row_table,
        saved_inputs.reshape(n_micro * tok_dev, dk, LANES),
        top_grad.reshape(n_micro, tok_dev, dk, LANES),
        meta,
        left_proj[0].T,
        gate_weight[0],
        up_weight[0],
        down_weight[0],
        right_proj[0].T,
    )
    return (
        grads.reshape(1, n_micro, tok_dev, feat),
        sketch.reshape(1, q_dev, r_dim * r_dim),
    )


def solution(mesh):
    placed = (
        P("section", None, "expert", None),
        P(None, "expert", None),
        P("section", None, "expert", None),
        P("section", None, "expert", None),
        P(None, "expert"),
        P("section", "expert", None),
        P("section", "expert", None),
        P("section", "expert", None),
        P("section", "expert", None),
        P("section", None, None),
    )
    return jax.shard_map(
        on_device,
        mesh=mesh,
        in_specs=placed,
        out_specs=(P("section", None, "expert", None), P("section", "expert", None)),
        check_vma=False,
    )
```

time: 1130 us -> 416 us (0.37); the launches traced: 1110 us -> 416 us
  waiting for transfers between devices: 520 us -> 0.01 us
  Pallas kernels: 0 us -> 401 us
  starting transfers between devices: 306 us -> 1.29 us
  other arithmetic: 96.1 us -> 1.17 us
  matrix products: 78.9 us -> 0 us
  local copies, waits for them, and re-layouts: 78.3 us -> 11.1 us
  blocking collectives: 30.7 us -> 0 us
    pallas_call x0 -> x1, Pallas kernels: none -> 401 us  [on_device(): pl.pallas_call(functools.partial(kernel, n_section, n_expert, groups), ou...]
    all_to_all x35 -> x0, waiting for transfers between devices: 397 us -> none  [the longest x17 204 us: sent_together(): lax.all_to_all(both, axis, split_axis=split_dim, concat_axis=concat_dim,...]
    all_to_all x35 -> x0, starting transfers between devices: 284 us -> none  [the longest x17 144 us: sent_together(): lax.all_to_all(both, axis, split_axis=split_dim, concat_axis=concat_dim,...]
    ppermute x17 -> x1, waiting for transfers between devices: 123 us -> 0.01 us  [on_device(): lax.ppermute(row_flat, 'section', [(i, i - 1) for i in range(1, n_section)])]
    dot_general x96 -> x0, matrix products: 78.9 us -> none  [the longest x17 20.9 us: one_step(): jnp.dot(out_grad, proj_right, preferred_element_type=jnp.float32)]
    add x36 -> x3, other arithmetic: 39.2 us -> 0.01 us  [the longest x2 0.01 us: on_device(): row_of = ids * (hsplit * CAP) + position]
    all_to_all x1 -> x0, blocking collectives: 30.7 us -> none  [sent_and_summed(): lax.all_to_all(blocks, axis, split_axis=0, concat_axis=0, tiled=True)]
    select_n x34 -> x0, local copies, waits for them, and re-layouts: 21.3 us -> none  [one_step(): jnp.where(is_live, contrib.reshape(q_total, sketch_dim * sketch_dim), jnp...]
  transfers between devices with their start and end apart: 52 -> 1, of which waited for: 52 -> 0; matrix products, arithmetic and copies ran while one was open for 5% -> 2% of each run, Pallas kernels for 0% -> 0%
where the time goes in v1:
time: 416 us
  Pallas kernels  401 us (96%)
  local copies, waits for them, and re-layouts  11.1 us (3%)
    pallas_call x1, Pallas kernels, on_device(): pl.pallas_call(functools.partial(kernel, n_section, n_expert, groups), ou...  401 us
  transfers between devices with their start and end apart: 1, of which 0 were waited for; matrix products, arithmetic and copies ran while one was open for 2% of the time, Pallas kernels for 0%

profile of v1, /device:TPU:6, one launch (start us, length us, event | category | flops | bytes accessed | tf_op | source)
XLA Modules:
  0.0 415.6 jit_solution(6432025366110802632)
XLA Ops:
  0.6 0.7 broadcast_multiply_fusion
  1.3 0.8 copy.39
  2.1 0.1 copy.40
  2.2 0.1 mul.34
  2.3 0.2 convert_reduce_fusion
  2.5 0.1 reduce_sum.42
  2.6 1.3 collective-permute-start
  3.9 0.1 mul.35
  4.1 0.8 copy.43
  4.9 0.1 reshape.122
  5.0 0.8 broadcast_in_dim.67
  5.7 0.1 broadcast_in_dim.68
  5.8 0.1 select_reduce_fusion
  5.9 0.1 select_reduce_fusion.1
  6.0 0.6 reshape.115.tok_ref
  6.7 0.1 copy.42
  6.8 0.1 copy.44
  7.1 0.6 copy.45
  7.7 1.5 copy.47
  9.2 1.5 copy.50
  10.7 0.7 copy.46.row_ref
  11.4 401.3 %shard_map.113 = (bf16[2,8,16,128]{3,2,1,0:T(8,128)(2,1)}, f32[2,32,128]{2,1,0:T(8,128)}) custom-call(s32[48]{0:T(128)} %reshape.115.tok_ref, s32[32,2]{1,0:T(8,128)} %copy.46.row_ref, bf16[16,16,128]{2,1,0:T(8,128)(2,1)} %bitcast.42, bf16[2,8,16,128]{3,2,1,0:T(8,128)(2,1)} %copy.50, f32[128,128]{1,0:T(8,128)} %bitcast.41, bf16[64,384]{1,0:T(8,128)(2,1)} %bitcast.47, ...), custom_call_target="tpu_custom_call" | custom-call | tf_op jit(solution)/shard_map/pallas_call | solution.py:465
  412.7 1.5 reshape.120
  414.2 1.4 reshape.121
  (15 shorter events, 0.5 us)
Async XLA Ops:
  2.6 8.0 %collective-permute-start = (s32[32]{0:T(128)S(1)}, s32[32]{0:T(128)S(1)}, u32[]{:S(2)}, u32[]{:S(2)}) collective-permute-start(s32[32]{0:T(128)S(1)} %add.33), channel_id=1, source_target_pairs={{32,0},{64,32},{96,64},{128,96},{160,128},{192,160},{224,192},{256... | collective-permute-start | bytes 392 | tf_op jit(solution)/shard_map/ppermute | solution.py:457

commit v2 on v1

--- a/solution.py
+++ b/solution.py
@@ -10,10 +10,23 @@
 EXPERTS = 8
 EXM = 4
 CAP = 3
+RING = 8
 LANES = 128
 F32 = jnp.float32
 BF16 = jnp.bfloat16
 MESH = pl.DeviceIdType.MESH
+
+
+def far_first(n, me, n_expert):
+    ring = RING if n_expert % RING == 0 else n_expert
+    across = n_expert // ring
+
+    def offset(rank, size):
+        return size // 2 + (1 - 2 * lax.rem(rank, 2)) * ((rank + 1) // 2)
+
+    z = lax.rem(lax.rem(me, ring) + offset(n // across, ring), ring)
+    x = lax.rem(me // ring + offset(lax.rem(n, across), across), across)
+    return x * ring + z
 
 
 def kernel(
@@ -100,7 +113,7 @@
 
     def greet(other, skip_me):
         def one(n, carry):
-            to = lax.rem(me + 1 + n, n_expert)
+            to = far_first(n, me, n_expert)
             pl.semaphore_signal(
                 barrier, inc=1, device_id={"section": other, "expert": to}, device_id_type=MESH
             )
@@ -134,7 +147,7 @@
 
     def spread(src, per, dst, send_sem, recv_sem):
         def one(n, carry):
-            to = lax.rem(me + 1 + n, n_expert)
+            to = far_first(n, me, n_expert)
             pltpu.make_async_remote_copy(
                 src_ref=src.at[pl.ds((to // hsplit) * per, per)],
                 dst_ref=dst.at[pl.ds(me * per, per)],
@@ -245,11 +258,13 @@
         coef_u[m] = weight * silu
         return carry
 
-    lax.fori_loop(0, n_micro, forward, 0)
+    @pl.when(jnp.logical_not(last))
+    def _():
+        lax.fori_loop(0, n_micro, forward, 0)
 
     def to_homes(m, other, skip_me, dst, recv_sem):
         def one(n, carry):
-            to = lax.rem(me + 1 + n, n_expert)
+            to = far_first(n, me, n_expert)
             pltpu.make_async_remote_copy(
                 src_ref=osend.at[m, pl.ds(to * CAP, CAP)],
                 dst_ref=dst.at[pl.ds(me * CAP, CAP)],
@@ -282,21 +297,29 @@
             copies.append((to, far, near))
         return copies
 
+    def home(m, carry):
+        await_all(resid.at[m], rr_sem.at[m])
+        for which in range(n_micro):
+
+            @pl.when(m == which)
+            def _():
+                await_all(crecv[which], cr_sem.at[which])
+                for t in range(tok_dev):
+                    base = resid[which, t].astype(F32)
+                    total = combined(which, t, base, crecv[which], 0)
+                    outgrad[which, t] = total.astype(BF16)
+
+        dispatch(m)
+        return carry
+
+    @pl.when(jnp.logical_not(last))
+    def _():
+        lax.fori_loop(0, n_micro, home, 0)
+
     def step(m, carry):
-        @pl.when(jnp.logical_not(last))
-        def _():
-            await_all(resid.at[m], rr_sem.at[m])
-            for which in range(n_micro):
-
-                @pl.when(m == which)
-                def _():
-                    await_all(crecv[which], cr_sem.at[which])
-                    for t in range(tok_dev):
-                        base = resid[which, t].astype(F32)
-                        total = combined(which, t, base, crecv[which], 0)
-                        outgrad[which, t] = total.astype(BF16)
-
-            dispatch(m)
+        @pl.when(last)
+        def _():
+            forward(m, 0)
 
         await_all(grecv.at[m], gr_sem.at[m])
         by_row(grecv, m)

time: 416 us -> 399 us (0.959)
  Pallas kernels: 401 us -> 385 us
    pallas_call x1, Pallas kernels: 401 us -> 385 us  [on_device(): pl.pallas_call(functools.partial(kernel, n_section, n_expert, groups), ou...]
where the time goes in v2:
time: 399 us
  Pallas kernels  385 us (96%)
  local copies, waits for them, and re-layouts  11.1 us (3%)
    pallas_call x1, Pallas kernels, on_device(): pl.pallas_call(functools.partial(kernel, n_section, n_expert, groups), ou...  385 us
  transfers between devices with their start and end apart: 1, of which 0 were waited for; matrix products, arithmetic and copies ran while one was open for 2% of the time, Pallas kernels for 0%

profile of v2, /device:TPU:6, one launch (start us, length us, event | category | flops | bytes accessed | tf_op | source)
XLA Modules:
  0.0 399.0 jit_solution(6145915195094078522)
XLA Ops:
  0.6 0.7 broadcast_multiply_fusion
  1.3 0.8 copy.39
  2.1 0.1 copy.40
  2.2 0.1 mul.34
  2.3 0.2 convert_reduce_fusion
  2.5 0.1 reduce_sum.42
  2.6 1.3 collective-permute-start
  3.9 0.1 mul.35
  4.0 0.1 reduce_sum.43
  4.1 0.8 copy.43
  4.9 0.1 reshape.122
  5.0 0.8 broadcast_in_dim.67
  5.8 0.1 select_reduce_fusion
  5.9 0.1 select_reduce_fusion.1
  6.0 0.6 reshape.115.tok_ref
  6.7 0.1 copy.42
  6.8 0.1 copy.44
  7.1 0.6 copy.45
  7.7 1.5 copy.47
  9.2 1.5 copy.50
  10.7 0.7 copy.46.row_ref
  11.4 384.7 %shard_map.113 = (bf16[2,8,16,128]{3,2,1,0:T(8,128)(2,1)}, f32[2,32,128]{2,1,0:T(8,128)}) custom-call(s32[48]{0:T(128)} %reshape.115.tok_ref, s32[32,2]{1,0:T(8,128)} %copy.46.row_ref, bf16[16,16,128]{2,1,0:T(8,128)(2,1)} %bitcast.42, bf16[2,8,16,128]{3,2,1,0:T(8,128)(2,1)} %copy.50, f32[128,128]{1,0:T(8,128)} %bitcast.41, bf16[64,384]{1,0:T(8,128)(2,1)} %bitcast.47, ...), custom_call_target="tpu_custom_call" | custom-call | tf_op jit(solution)/shard_map/pallas_call | solution.py:488
  396.1 1.5 reshape.120
  397.6 1.4 reshape.121
  (15 shorter events, 0.5 us)
Async XLA Ops:
  2.6 8.0 %collective-permute-start = (s32[32]{0:T(128)S(1)}, s32[32]{0:T(128)S(1)}, u32[]{:S(2)}, u32[]{:S(2)}) collective-permute-start(s32[32]{0:T(128)S(1)} %add.33), channel_id=1, source_target_pairs={{32,0},{64,32},{96,64},{128,96},{160,128},{192,160},{224,192},{256... | collective-permute-start | bytes 392 | tf_op jit(solution)/shard_map/ppermute | solution.py:480

commit v3 on v2

--- a/solution.py
+++ b/solution.py
@@ -47,6 +47,7 @@
     sketch_ref,
     wgu,
     wdr,
+    xrows,
     xsend,
     xrecv,
     gsend,
@@ -57,6 +58,7 @@
     frecv_a,
     frecv_b,
     metar,
+    metaw,
     outgrad,
     resid,
     back,
@@ -66,6 +68,7 @@
     coef_g,
     coef_u,
     left_keep,
+    right_keep,
     psend,
     srecv,
     w_sem,
@@ -89,11 +92,10 @@
     sec = lax.axis_index("section")
     me = lax.axis_index("expert")
     hsplit = n_expert // groups
-    n_micro, tok_dev = top_ref.shape[:2]
+    n_micro, tok_dev, dk, _ = outgrad.shape
     n_slots = groups * CAP
-    dk = x_ref.shape[1]
     hid = down_hbm.shape[0]
-    top_k = row_ref.shape[0] // (n_micro * tok_dev)
+    top_k = row_ref.shape[0] // (2 * n_micro * tok_dev)
     q_dev = n_micro * EXM * groups // n_expert
     r_dim = left_ref.shape[0]
     half = r_dim // 2
@@ -131,9 +133,21 @@
     def _():
         greet(sec + 1, False)
 
+    def tiles_of(ref):
+        n = n_micro * tok_dev
+        for k in range(dk):
+            wide[pl.ds(k, n, stride=dk), :] = ref[:, pl.ds(k * LANES, LANES)].astype(F32)
+        return wide[pl.ds(0, n * dk), :].astype(BF16).reshape(n, dk, LANES)
+
+    xrows[...] = tiles_of(x_ref)
+
+    @pl.when(last)
+    def _():
+        outgrad[...] = tiles_of(top_ref).reshape(n_micro, tok_dev, dk, LANES)
+
     def xbuild(m, carry):
         for s in range(n_slots):
-            xsend[m, s] = x_ref[m * tok_dev + tok_ref[m * n_slots + s]]
+            xsend[m, s] = xrows[m * tok_dev + tok_ref[m * n_slots + s]]
         return carry
 
     lax.fori_loop(0, n_micro, xbuild, 0)
@@ -158,7 +172,8 @@
             ).start()
             return carry
 
-        lax.fori_loop(0, n_expert - 1, one, 0)
+        for n in range(n_expert - 1):
+            one(n, 0)
         pltpu.make_async_copy(
             src.at[pl.ds((me // hsplit) * per, per)], dst.at[pl.ds(me * per, per)], recv_sem
         ).start()
@@ -196,26 +211,28 @@
     def combined(m, t, base, parts, which):
         total = base
         for k in range(top_k):
-            at = row_ref[m * tok_dev * top_k + t * top_k + k, which]
+            at = row_ref[((which * n_micro + m) * top_k + k) * tok_dev + t]
             for j in range(hsplit):
                 total = total + parts[at + j * CAP].astype(F32)
         return total
 
-    def start_micro(m, carry):
+    def send_inputs(m):
         spread(xsend.at[m], CAP, xrecv.at[m], xs_sem.at[m], xr_sem.at[m])
 
-        @pl.when(m == 0)
-        def _():
-            spread(meta_ref, 16, metar, ms_sem, mr_sem)
-
-        @pl.when(last)
-        def _():
-            outgrad[m] = top_ref[m]
+    send_inputs(0)
+    spread(meta_ref, 16, metar, ms_sem, mr_sem)
+
+    @pl.when(last)
+    def _():
+        def start_micro(m, carry):
+            @pl.when(m > 0)
+            def _():
+                send_inputs(m)
+
             dispatch(m)
-
-        return carry
-
-    lax.fori_loop(0, n_micro, start_micro, 0)
+            return carry
+
+        lax.fori_loop(0, n_micro, start_micro, 0)
 
     def by_row(ref, m):
         wide[...] = ref[m].reshape(n_expert * CAP * dk, LANES).astype(F32)
@@ -229,7 +246,7 @@
         return jnp.concatenate(
             [
                 jnp.concatenate(
-                    [metar[pl.ds(b * 8 + m * 4 + c, n_expert, stride=16), :] for b in range(2)],
+                    [metaw[pl.ds(b * 8 + m * 4 + c, n_expert, stride=16), :] for b in range(2)],
                     axis=1,
                 )
                 for c in range(CAP)
@@ -241,6 +258,7 @@
     for load in loads:
         load.wait()
     await_all(metar, mr_sem)
+    metaw[...] = metar[...].astype(F32)
 
     def forward(m, carry):
         await_all(xrecv.at[m], xr_sem.at[m])
@@ -260,7 +278,16 @@
 
     @pl.when(jnp.logical_not(last))
     def _():
-        lax.fori_loop(0, n_micro, forward, 0)
+        def prepare(m, carry):
+            forward(m, 0)
+
+            @pl.when(m + 1 < n_micro)
+            def _():
+                send_inputs(m + 1)
+
+            return carry
+
+        lax.fori_loop(0, n_micro, prepare, 0)
 
     def to_homes(m, other, skip_me, dst, recv_sem):
         def one(n, carry):
@@ -275,7 +302,8 @@
             ).start()
             return carry
 
-        lax.fori_loop(0, n_expert - 1 if skip_me else n_expert, one, 0)
+        for n in range(n_expert - 1 if skip_me else n_expert):
+            one(n, 0)
 
     def sketch_copies(m):
         mine = me // hsplit
@@ -356,7 +384,11 @@
             def _():
                 to_homes(which, sec - 1, False, crecv[which], cr_sem.at[which])
 
-        right = jnp.concatenate([right] * EXM, axis=1) * meta_of(m)
+        right_keep[m] = right
+        return carry
+
+    def outer_of(m, carry):
+        right = jnp.concatenate([right_keep[m]] * EXM, axis=1) * meta_of(m)
         left = left_keep[m].astype(BF16)
         at_r = lax.broadcasted_iota(jnp.int32, (r_dim, r_dim), 0)
         at_c = lax.broadcasted_iota(jnp.int32, (r_dim, r_dim), 1)
@@ -382,6 +414,7 @@
         return carry
 
     lax.fori_loop(0, n_micro, step, 0)
+    lax.fori_loop(0, n_micro, outer_of, 0)
 
     @pl.when(first)
     def _():
@@ -455,8 +488,8 @@
     r_dim = left_proj.shape[2]
     q_dev = n_micro * EXM * groups // n_expert
 
-    ids = expert_ids[0].reshape(n_micro, n_pairs)
-    weights = route_weights[0].reshape(n_micro, n_pairs).astype(F32)
+    ids = expert_ids[0].swapaxes(1, 2).reshape(n_micro, n_pairs)
+    weights = route_weights[0].swapaxes(1, 2).reshape(n_micro, n_pairs).astype(F32)
     pair = jnp.arange(n_pairs, dtype=jnp.int32)
     same = (ids[:, :, None] == ids[:, None, :]) & (pair[:, None] > pair[None, :])[None]
     position = jnp.sum(same.astype(jnp.int32), axis=2)
@@ -464,9 +497,9 @@
     row_of = ids * (hsplit * CAP) + position
     slots = jnp.arange(n_slots, dtype=jnp.int32)
     select = slot_of[:, None, :] == slots[None, :, None]
-    tok_of_slot = jnp.sum(jnp.where(select, (pair // top_k)[None, None], 0), axis=2)
+    tok_of_slot = jnp.sum(jnp.where(select, (pair % tok_dev)[None, None], 0), axis=2)
     slot_weight = jnp.sum(jnp.where(select, weights[:, None, :], 0.0), axis=2)
-    example_pairs = jnp.repeat(example_ids, top_k, axis=1)
+    example_pairs = jnp.concatenate([example_ids] * top_k, axis=1)
     slot_example = jnp.sum(jnp.where(select, example_pairs[:, None, :], 0), axis=2)
     lane_example = jnp.arange(EXM * r_dim, dtype=jnp.int32) // r_dim
     meta = jnp.where(
@@ -475,10 +508,10 @@
     meta = meta.reshape(n_micro, groups, CAP, EXM * r_dim).swapaxes(0, 1)
     meta = jnp.pad(meta, ((0, 0), (0, 0), (0, 4 - CAP), (0, 0)))
     meta = meta.reshape(groups, n_micro * 4, 2, LANES).swapaxes(1, 2)
-    meta = meta.reshape(groups * 2 * n_micro * 4, LANES)
+    meta = meta.reshape(groups * 2 * n_micro * 4, LANES).astype(BF16)
     row_flat = row_of.reshape(n_micro * n_pairs)
     above = lax.ppermute(row_flat, "section", [(i, i - 1) for i in range(1, n_section)])
-    row_table = jnp.stack([above, row_flat], axis=1)
+    row_table = jnp.concatenate([above, row_flat])
 
     n_rows = n_expert * CAP
     vmem = pl.BlockSpec(memory_space=pltpu.VMEM)
@@ -496,6 +529,7 @@
         scratch_shapes=[
             pltpu.VMEM((2 * hid, feat), BF16),
             pltpu.VMEM((hid + r_dim, feat), BF16),
+            pltpu.VMEM((n_micro * tok_dev, dk, LANES), BF16),
             pltpu.VMEM((n_micro, n_slots, dk, LANES), BF16),
             pltpu.VMEM((n_micro, n_rows, dk, LANES), BF16),
             pltpu.VMEM((n_micro, n_slots, dk, LANES), BF16),
@@ -505,6 +539,7 @@
             pltpu.VMEM((n_rows, dk, LANES), BF16),
             pltpu.VMEM((n_rows, dk, LANES), BF16),
             pltpu.VMEM((n_rows, dk, LANES), BF16),
+            pltpu.VMEM((n_expert * 16, LANES), BF16),
             pltpu.VMEM((n_expert * 16, LANES), F32),
             pltpu.VMEM((n_micro, tok_dev, dk, LANES), BF16),
             pltpu.VMEM((n_micro, tok_dev, dk, LANES), BF16),
@@ -515,6 +550,7 @@
             pltpu.VMEM((n_micro, n_rows, hid), F32),
             pltpu.VMEM((n_micro, n_rows, hid), F32),
             pltpu.VMEM((n_micro, n_rows, r_dim), F32),
+            pltpu.VMEM((n_micro, n_rows, r_dim), F32),
             pltpu.VMEM((n_micro, EXM, r_dim // 2, 2 * r_dim), F32),
             pltpu.VMEM((q_dev, hsplit, r_dim // 2, 2 * r_dim), F32),
             dma((4,)),
@@ -538,8 +574,8 @@
     )(
         tok_of_slot.reshape(n_micro * n_slots),
         row_table,
-        saved_inputs.reshape(n_micro * tok_dev, dk, LANES),
-        top_grad.reshape(n_micro, tok_dev, dk, LANES),
+        saved_inputs.reshape(n_micro * tok_dev, feat),
+        top_grad.reshape(n_micro * tok_dev, feat),
         meta,
         left_proj[0].T,
         gate_weight[0],

time: 399 us -> 377 us (0.945)
  Pallas kernels: 385 us -> 366 us
  local copies, waits for them, and re-layouts: 11.1 us -> 5.51 us
    pallas_call x1, Pallas kernels: 385 us -> 366 us  [on_device(): pl.pallas_call(functools.partial(kernel, n_section, n_expert, groups), ou...]
  transfers between devices with their start and end apart: 1 -> 1, of which waited for: 0 -> 0; matrix products, arithmetic and copies ran while one was open for 2% -> 1% of each run, Pallas kernels for 0% -> 0%
where the time goes in v3:
time: 377 us
  Pallas kernels  366 us (97%)
  local copies, waits for them, and re-layouts  5.51 us (1%)
    pallas_call x1, Pallas kernels, on_device(): pl.pallas_call(functools.partial(kernel, n_section, n_expert, groups), ou...  366 us
  transfers between devices with their start and end apart: 1, of which 0 were waited for; matrix products, arithmetic and copies ran while one was open for 1% of the time, Pallas kernels for 0%

profile of v3, /device:TPU:6, one launch (start us, length us, event | category | flops | bytes accessed | tf_op | source)
XLA Modules:
  0.0 376.7 jit_solution(5818866347179430608)
XLA Ops:
  0.6 0.7 broadcast_multiply_fusion
  1.3 0.8 reshape.93
  2.1 0.1 mul.24
  2.2 0.2 convert_reduce_fusion
  2.4 0.1 reduce_sum.40
  2.4 1.3 collective-permute-start
  3.8 0.8 pad_add_fusion
  4.6 0.7 convert_bitcast_fusion
  5.3 0.1 reshape.99
  5.4 0.1 select_reduce_fusion
  5.5 0.1 select_reduce_fusion.1
  5.6 0.6 reshape.94.tok_ref
  6.2 0.1 broadcast_in_dim.66
  6.2 0.1 copy.18
  6.3 0.1 eq.53
  6.4 0.1 copy.17
  6.5 0.1 select_convert_fusion
  6.6 0.6 copy.19
  7.3 0.0 collective-permute-done
  7.3 0.6 pad_add_fusion.1.row_ref
  7.8 366.0 %shard_map.113 = (bf16[2,8,16,128]{3,2,1,0:T(8,128)(2,1)}, f32[2,32,128]{2,1,0:T(8,128)}) custom-call(s32[48]{0:T(128)} %reshape.94.tok_ref, s32[64]{0:T(128)} %pad_add_fusion.1.row_ref, bf16[16,2048]{1,0:T(8,128)(2,1)} %bitcast.36, bf16[16,2048]{1,0:T(8,128)(2,1)} %bitcast.37, bf16[128,128]{1,0:T(8,128)(2,1)} %bitcast.34, bf16[64,384]{1,0:T(8,128)(2,1)} %bitcast.38, ...), custom_call_target="tpu_custom_call" | custom-call | tf_op jit(solution)/shard_map/pallas_call | solution.py:521
  373.8 1.5 reshape.97
  375.3 1.4 reshape.98
  (7 shorter events, 0.1 us)
Async XLA Ops:
  2.4 4.8 %collective-permute-start = (s32[32]{0:T(128)S(1)}, s32[32]{0:T(128)S(1)}, u32[]{:S(2)}, u32[]{:S(2)}) collective-permute-start(s32[32]{0:T(128)S(1)} %add.30), channel_id=1, source_target_pairs={{32,0},{64,32},{96,64},{128,96},{160,128},{192,160},{224,192},{256... | collective-permute-start | bytes 392 | tf_op jit(solution)/shard_map/ppermute | solution.py:513

commit v4 on v3

--- a/solution.py
+++ b/solution.py
@@ -24,8 +24,8 @@
     def offset(rank, size):
         return size // 2 + (1 - 2 * lax.rem(rank, 2)) * ((rank + 1) // 2)
 
-    z = lax.rem(lax.rem(me, ring) + offset(n // across, ring), ring)
-    x = lax.rem(me // ring + offset(lax.rem(n, across), across), across)
+    z = lax.rem(lax.rem(me, ring) + offset(lax.rem(n, ring), ring), ring)
+    x = lax.rem(me // ring + offset(n // ring, across), across)
     return x * ring + z
 
 

time: 377 us -> 368 us (0.976)
  Pallas kernels: 366 us -> 357 us
    pallas_call x1, Pallas kernels: 366 us -> 357 us  [on_device(): pl.pallas_call(functools.partial(kernel, n_section, n_expert, groups), ou...]
where the time goes in v4:
time: 368 us; the launch traced here: 367 us
  Pallas kernels  357 us (97%)
  local copies, waits for them, and re-layouts  5.51 us (1%)
    pallas_call x1, Pallas kernels, on_device(): pl.pallas_call(functools.partial(kernel, n_section, n_expert, groups), ou...  357 us
  transfers between devices with their start and end apart: 1, of which 0 were waited for; matrix products, arithmetic and copies ran while one was open for 1% of the time, Pallas kernels for 0%

profile of v4, /device:TPU:6, one launch (start us, length us, event | category | flops | bytes accessed | tf_op | source)
XLA Modules:
  0.0 367.4 jit_solution(15507506906935970614)
XLA Ops:
  0.6 0.7 broadcast_multiply_fusion
  1.3 0.8 reshape.93
  2.1 0.1 mul.24
  2.2 0.2 convert_reduce_fusion
  2.4 0.1 reduce_sum.40
  2.4 1.3 collective-permute-start
  3.8 0.8 pad_add_fusion
  4.6 0.7 convert_bitcast_fusion
  5.3 0.1 reshape.99
  5.4 0.1 select_reduce_fusion
  5.5 0.1 select_reduce_fusion.1
  5.6 0.6 reshape.94.tok_ref
  6.2 0.1 broadcast_in_dim.66
  6.2 0.1 copy.18
  6.3 0.1 eq.53
  6.4 0.1 copy.17
  6.5 0.1 select_convert_fusion
  6.6 0.6 copy.19
  7.3 0.0 collective-permute-done
  7.3 0.6 pad_add_fusion.1.row_ref
  7.8 356.7 %shard_map.113 = (bf16[2,8,16,128]{3,2,1,0:T(8,128)(2,1)}, f32[2,32,128]{2,1,0:T(8,128)}) custom-call(s32[48]{0:T(128)} %reshape.94.tok_ref, s32[64]{0:T(128)} %pad_add_fusion.1.row_ref, bf16[16,2048]{1,0:T(8,128)(2,1)} %bitcast.36, bf16[16,2048]{1,0:T(8,128)(2,1)} %bitcast.37, bf16[128,128]{1,0:T(8,128)(2,1)} %bitcast.34, bf16[64,384]{1,0:T(8,128)(2,1)} %bitcast.38, ...), custom_call_target="tpu_custom_call" | custom-call | tf_op jit(solution)/shard_map/pallas_call | solution.py:521
  364.5 1.5 reshape.97
  366.0 1.4 reshape.98
  (7 shorter events, 0.1 us)
Async XLA Ops:
  2.4 4.8 %collective-permute-start = (s32[32]{0:T(128)S(1)}, s32[32]{0:T(128)S(1)}, u32[]{:S(2)}, u32[]{:S(2)}) collective-permute-start(s32[32]{0:T(128)S(1)} %add.30), channel_id=1, source_target_pairs={{32,0},{64,32},{96,64},{128,96},{160,128},{192,160},{224,192},{256... | collective-permute-start | bytes 392 | tf_op jit(solution)/shard_map/ppermute | solution.py:513

commit v5 on v4

--- a/solution.py
+++ b/solution.py
@@ -115,7 +115,7 @@
 
     def greet(other, skip_me):
         def one(n, carry):
-            to = far_first(n, me, n_expert)
+            to = lax.rem(me + 1 + n, n_expert)
             pl.semaphore_signal(
                 barrier, inc=1, device_id={"section": other, "expert": to}, device_id_type=MESH
             )

time: 368 us -> 365 us (level)
  no operation moved by 1% of the time
where the time goes in v5:
time: 365 us
  Pallas kernels  354 us (97%)
  local copies, waits for them, and re-layouts  5.51 us (2%)
    pallas_call x1, Pallas kernels, on_device(): pl.pallas_call(functools.partial(kernel, n_section, n_expert, groups), ou...  354 us
  transfers between devices with their start and end apart: 1, of which 0 were waited for; matrix products, arithmetic and copies ran while one was open for 1% of the time, Pallas kernels for 0%

profile of v5, /device:TPU:6, one launch (start us, length us, event | category | flops | bytes accessed | tf_op | source)
XLA Modules:
  0.0 365.1 jit_solution(13669711616194063765)
XLA Ops:
  0.6 0.7 broadcast_multiply_fusion
  1.3 0.8 reshape.93
  2.1 0.1 mul.24
  2.2 0.2 convert_reduce_fusion
  2.4 0.1 reduce_sum.40
  2.4 1.3 collective-permute-start
  3.8 0.8 pad_add_fusion
  4.6 0.7 convert_bitcast_fusion
  5.3 0.1 reshape.99
  5.4 0.1 select_reduce_fusion
  5.5 0.1 select_reduce_fusion.1
  5.6 0.6 reshape.94.tok_ref
  6.2 0.1 broadcast_in_dim.66
  6.2 0.1 copy.18
  6.3 0.1 eq.53
  6.4 0.1 copy.17
  6.5 0.1 select_convert_fusion
  6.6 0.6 copy.19
  7.3 0.0 collective-permute-done
  7.3 0.6 pad_add_fusion.1.row_ref
  7.8 354.4 %shard_map.113 = (bf16[2,8,16,128]{3,2,1,0:T(8,128)(2,1)}, f32[2,32,128]{2,1,0:T(8,128)}) custom-call(s32[48]{0:T(128)} %reshape.94.tok_ref, s32[64]{0:T(128)} %pad_add_fusion.1.row_ref, bf16[16,2048]{1,0:T(8,128)(2,1)} %bitcast.36, bf16[16,2048]{1,0:T(8,128)(2,1)} %bitcast.37, bf16[128,128]{1,0:T(8,128)(2,1)} %bitcast.34, bf16[64,384]{1,0:T(8,128)(2,1)} %bitcast.38, ...), custom_call_target="tpu_custom_call" | custom-call | tf_op jit(solution)/shard_map/pallas_call | solution.py:521
  362.2 1.5 reshape.97
  363.7 1.4 reshape.98
  (7 shorter events, 0.1 us)
Async XLA Ops:
  2.4 4.8 %collective-permute-start = (s32[32]{0:T(128)S(1)}, s32[32]{0:T(128)S(1)}, u32[]{:S(2)}, u32[]{:S(2)}) collective-permute-start(s32[32]{0:T(128)S(1)} %add.30), channel_id=1, source_target_pairs={{32,0},{64,32},{96,64},{128,96},{160,128},{192,160},{224,192},{256... | collective-permute-start | bytes 392 | tf_op jit(solution)/shard_map/ppermute | solution.py:513
